TPU v7x, 32 devices: a whole 2x2x4 slice. The times are simulated.
32 devices in a mesh: region: 8 (over z, y), member: 4 (over x, core).
Axes of the slice: x: 2, y: 2, z: 4, core: 2. Of those that a mesh axis runs over, the one named last changes fastest.
Arguments:
- ensemble: bfloat16 [256, 16384], P('member', 'region'), may hold values from -6 to 6
- reports: float32 [8, 1024], P('region'), may hold values from -6 to 6
- report_count: int32 [8], P('region'), may hold values from 128 to 1024, as said below
- report_cell: int32 [8, 1024], P('region'), may hold values from 0 to 16383, as said below
- report_weight: float32 [8, 16, 1024], P('region', 'member'), may hold values from 0.001 to 1
- blending: float32 [4, 16384], P(None, ('region', 'member')), may hold values from 0.02 to 1
Outputs:
- analysis: bfloat16 [16384, 256], P(('region', 'member'))
Inputs may be any that keep to these rules, and one draw needn't show every extreme that they name: `report_count`: the largest value 1024 is reached by some region in every draw. `report_cell`: every cell lies in the slot's own region, or in the first 128 cells of one of at most two other regions chosen for that region.
All inputs are finite; a program needn't handle non-finite values.
Results may differ from a plain program's by a relative error of at most 0.0055.
Values may be sent and summed in bfloat16 or wider, within the bound.
No kernel may reach another device: no remote copies, remote signals or barrier semaphores. Data moves between devices by JAX's collectives and lax.ppermute only.
A program may use at most 64 MiB of HBM per device.

v0:
```python
import jax
import jax.numpy as jnp
from jax import lax
from jax.sharding import PartitionSpec as P

MARGIN = 128
SWEEPS = 4
highest = lax.Precision.HIGHEST


def extended(block, sides, width):
    for axis, dim in sides:
        count = lax.axis_size(axis)
        forward = [(i, i + 1) for i in range(count - 1)]
        backward = [(target, source) for source, target in forward]
        low = lax.ppermute(
            lax.slice_in_dim(block, block.shape[dim] - width, None, axis=dim), axis, forward
        )
        high = lax.ppermute(lax.slice_in_dim(block, 0, width, axis=dim), axis, backward)
        block = jnp.concatenate([low, block, high], axis=dim)
    return block


def make_transform(products, forcing, members):
    identity = jnp.eye(members, dtype=jnp.float32)
    precision_mat = (members - 1.0) * identity[None] + products
    frobenius = jnp.sqrt(jnp.sum(precision_mat * precision_mat, axis=(1, 2)))
    current = precision_mat / frobenius[:, None, None]
    root_iter = jnp.broadcast_to(identity, current.shape)
    for iteration in range(SWEEPS):
        middle = 1.5 * identity[None] - 0.5 * jnp.einsum(
            "aij,ajk->aik", root_iter, current, precision=highest
        )
        current = jnp.einsum("aij,ajk->aik", current, middle, precision=highest)
        root_iter = jnp.einsum("aij,ajk->aik", middle, root_iter, precision=highest)
    inverse_root = root_iter / jnp.sqrt(frobenius)[:, None, None]
    inner_step = jnp.einsum("aij,aj->ai", inverse_root, forcing, precision=highest)
    mean_weights = jnp.einsum("aij,aj->ai", inverse_root, inner_step, precision=highest)
    return (mean_weights[:, :, None] + jnp.sqrt(members - 1.0) * inverse_root).astype(jnp.bfloat16)


def corner_layout(band_index, points_here, row_count):
    group_index = jnp.arange(4 * points_here, dtype=jnp.int32)
    upper_half = group_index // (2 * points_here)
    column_block = group_index // 2 % points_here
    right_half = group_index % 2
    row_base = jnp.clip(band_index - 1 + upper_half, 0, row_count - 2)
    col_base = jnp.clip(column_block - 1 + right_half, 0, points_here - 2)
    return (row_base, col_base)


def per_device(ensemble, reports, report_count, report_cell, report_weight, blending):
    local_members, cell_count = ensemble.shape
    groups = lax.axis_size("member")
    members = local_members * groups
    region = lax.axis_index("region")
    member = lax.axis_index("member")
    targets = report_cell[0]
    holder = targets // cell_count
    within = targets % cell_count
    is_local = holder == region
    local_values = jnp.take(ensemble, jnp.where(is_local, within, 0), axis=1).astype(jnp.float32)
    border = ensemble[:, :MARGIN]
    border_index = holder * MARGIN + jnp.minimum(within, MARGIN - 1)
    pieces = lax.all_gather(border, "region", axis=1, tiled=True)
    extent = pieces.shape[1]
    inside = (border_index >= 0) & (border_index < extent) & jnp.logical_not(is_local)
    picked = jnp.take(pieces, jnp.clip(border_index, 0, extent - 1), axis=1).astype(jnp.float32)
    remote = jnp.where(inside[None, :], picked, 0.0)
    at_reports = jnp.where(is_local[None, :], local_values, remote)
    report_mean = lax.psum(jnp.sum(at_reports, axis=0), "member") / members
    local_pert = (at_reports - report_mean[None, :]).astype(jnp.bfloat16)
    report_pert = lax.all_gather(local_pert, "member", axis=0, tiled=True)
    active = (jnp.arange(report_pert.shape[1]) < report_count[0]).astype(jnp.float32)
    weights = report_weight[0] * active[None, :]
    weighted = (report_pert[None, :, :] * weights[:, None, :]).astype(jnp.bfloat16)
    departure = (weights * (reports[0] - report_mean)[None, :]).astype(jnp.bfloat16)
    products = jnp.einsum("ako,jo->akj", weighted, report_pert, preferred_element_type=jnp.float32)
    forcing = jnp.einsum("ao,ko->ak", departure, report_pert, preferred_element_type=jnp.float32)
    transform = make_transform(products, forcing, members)
    points_here = transform.shape[0]
    groups_band = 4 * points_here
    slab_cells = cell_count // groups
    group_cells = slab_cells // groups_band
    mixing = blending / jnp.sum(blending, axis=0, keepdims=True)
    columns = lax.all_to_all(ensemble, "member", split_axis=1, concat_axis=0, tiled=True)
    cell_mean = jnp.sum(columns, axis=0, dtype=jnp.float32) / members
    anomaly = (columns - cell_mean[None, :]).astype(jnp.bfloat16)
    anomaly_view = anomaly.reshape(members, groups_band, group_cells)
    mix_view = mixing.reshape(4, groups_band, group_cells)
    neighbours = extended(transform[None], (("member", 0),), 1)
    stacked = neighbours.reshape(3 * points_here, members, members)
    row_base, col_base = corner_layout(member, points_here, groups)
    running = jnp.zeros((groups_band, group_cells, members), jnp.float32)
    for corner in range(4):
        row_step = corner // 2
        col_step = corner % 2
        chosen_index = (row_base + row_step - (member - 1)) * points_here + col_base + col_step
        chosen = jnp.take(stacked, chosen_index, axis=0)
        spread = jnp.einsum(
            "kgc,gkj->gcj", anomaly_view, chosen, preferred_element_type=jnp.float32
        )
        running = running + mix_view[corner][:, :, None] * spread
    blended = running.reshape(slab_cells, members)
    return (cell_mean[:, None] + blended).astype(jnp.bfloat16)


def solution(mesh):
    return jax.shard_map(
        per_device,
        mesh=mesh,
        in_specs=(
            P("member", "region"),
            P("region", None),
            P("region"),
            P("region", None),
            P("region", "member", None),
            P(None, ("region", "member")),
        ),
        out_specs=P(("region", "member"), None),
        check_vma=False,
    )
```

profile of v0, /device:TPU:0, one launch (start us, length us, event | category | flops | bytes accessed | tf_op | source)
XLA Modules:
  0.0 104.7 jit_solution(4873198254214473473)
XLA Ops:
  1.6 1.2 %copy.24 = bf16[64,2048]{0,1:T(8,128)(2,1)S(1)} copy(bf16[64,2048]{1,0:T(8,128)(2,1)} %param.8) | data formatting | bytes 524288 | tf_op args[0]
  2.9 3.2 %gather_fusion = bf16[1024,64]{1,0:T(8,128)(2,1)S(1)} fusion(bf16[64,2048]{0,1:T(8,128)(2,1)S(1)} %copy.24, s32[1024]{0:T(1024)S(1)} %broadcast_clamp_fusion.1), kind=kCustom, calls=%fused_computation.4 | custom fusion | bytes 266240 | tf_op jit(solution)/shard_map/jit(_take)/gather | solution.py:62
  6.3 32.6 %all_gather.6 = bf16[64,1024]{0,1:T(8,128)(2,1)S(1)} all-gather(bf16[64,128]{0,1:T(8,128)(2,1)S(1)} %slice.37), channel_id=1, replica_groups=mesh['region'=8,'member'=4] {'region'}, dimensions={1}, use_global_device_ids=true | all-gather | bytes 147456 | tf_op jit(solution)/shard_map/all_gather | solution.py:65
  38.9 3.2 %gather_fusion.1 = bf16[1024,64]{1,0:T(8,128)(2,1)S(1)} fusion(bf16[64,1024]{0,1:T(8,128)(2,1)S(1)} %all_gather.6, s32[1024]{0:T(1024)S(1)} %broadcast_clamp_fusion), kind=kCustom, calls=%fused_computation.5 | custom fusion | bytes 266240 | tf_op jit(solution)/shard_map/jit(_take)/gather | solution.py:68
  42.3 5.7 %psum.7 = f32[1024]{0:T(1024)S(1)} all-reduce(f32[1024]{0:T(1024)S(1)} %fusion.54), channel_id=1, replica_groups=mesh['region'=8,'member'=4] {'member'}, use_global_device_ids=true, to_apply=%region_3.4 | all-reduce | flops 1024 | bytes 8192 | tf_op jit(solution)/shard_map/psum | solution.py:71
  48.1 7.4 %all_gather.7 = bf16[256,1024]{1,0:T(8,128)(2,1)S(1)} all-gather(bf16[64,1024]{1,0:T(8,128)(2,1)S(1)} %fusion.56), channel_id=1, replica_groups=mesh['region'=8,'member'=4] {'member'}, dimensions={0}, use_global_device_ids=true | all-gather | bytes 655360 | tf_op jit(solution)/shard_map/all_gather | solution.py:73
  57.2 1.2 %fusion.19 = f32[4,256,256]{2,1,0:T(8,128)S(1)} fusion(f32[256,256]{1,0:T(8,128)S(1)} %fusion.52, f32[256,256]{1,0:T(8,128)S(1)} %fusion.53, f32[4,256,256]{2,1,0:T(8,128)S(1)} %get-tuple-element.24, f32[4]{0:T(128)S(1)} %get-tuple-element.22), kind=kOutput, calls=%fused_computation.32 | convolution fusion | flops 806092800 | bytes 2621456 | tf_op jit(solution)/shard_map/aij,ajk->aik/dot_general | solution.py:31
  58.4 1.2 %fusion.55 = f32[4,256,256]{2,1,0:T(8,128)S(1)} fusion(f32[4,256,256]{2,1,0:T(8,128)S(1)} %fusion.19, f32[4,256,256]{2,1,0:T(8,128)S(1)} %get-tuple-element.24, f32[4]{0:T(128)S(1)} %get-tuple-element.22), kind=kOutput, calls=%fused_computation.66 | convolution fusion | flops 805568512 | bytes 3145744 | tf_op jit(solution)/shard_map/aij,ajk->aik/dot_general | solution.py:34
  60.7 1.2 %fusion.18 = f32[4,256,256]{2,1,0:T(8,128)S(1)} fusion(f32[4,256,256]{2,1,0:T(8,128)S(1)} %fusion.48, f32[4,256,256]{2,1,0:T(8,128)S(1)} %fusion.55, f32[256,256]{1,0:T(8,128)S(1)} %fusion.53), kind=kOutput, calls=%fused_computation.30 | convolution fusion | flops 805830656 | bytes 3407872 | tf_op jit(solution)/shard_map/aij,ajk->aik/dot_general | solution.py:31
  61.9 1.1 %fusion.79 = f32[4,256,256]{2,1,0:T(8,128)S(1)} fusion(f32[4,256,256]{2,1,0:T(8,128)S(1)} %fusion.55, f32[4,256,256]{2,1,0:T(8,128)S(1)} %fusion.18), kind=kOutput, calls=%fused_computation.158 | convolution fusion | flops 805306368 | bytes 3145728 | tf_op jit(solution)/shard_map/aij,ajk->aik/dot_general | solution.py:34
  63.0 1.1 %fusion.78 = f32[4,256,256]{2,1,0:T(8,128)S(1)} fusion(f32[4,256,256]{2,1,0:T(8,128)S(1)} %fusion.18, f32[4,256,256]{2,1,0:T(8,128)S(1)} %fusion.48), kind=kOutput, calls=%fused_computation.157 | convolution fusion | flops 805306368 | bytes 3145728 | tf_op jit(solution)/shard_map/aij,ajk->aik/dot_general | solution.py:35
  64.2 1.2 %fusion.17 = f32[4,256,256]{2,1,0:T(8,128)S(1)} fusion(f32[4,256,256]{2,1,0:T(8,128)S(1)} %fusion.78, f32[4,256,256]{2,1,0:T(8,128)S(1)} %fusion.79, f32[256,256]{1,0:T(8,128)S(1)} %fusion.53), kind=kOutput, calls=%fused_computation.28 | convolution fusion | flops 805830656 | bytes 3407872 | tf_op jit(solution)/shard_map/aij,ajk->aik/dot_general | solution.py:31
  65.4 1.1 %fusion.81 = f32[4,256,256]{2,1,0:T(8,128)S(1)} fusion(f32[4,256,256]{2,1,0:T(8,128)S(1)} %fusion.79, f32[4,256,256]{2,1,0:T(8,128)S(1)} %fusion.17), kind=kOutput, calls=%fused_computation.160 | convolution fusion | flops 805306368 | bytes 3145728 | tf_op jit(solution)/shard_map/aij,ajk->aik/dot_general | solution.py:34
  66.5 1.1 %fusion.80 = f32[4,256,256]{2,1,0:T(8,128)S(1)} fusion(f32[4,256,256]{2,1,0:T(8,128)S(1)} %fusion.17, f32[4,256,256]{2,1,0:T(8,128)S(1)} %fusion.78), kind=kOutput, calls=%fused_computation.159 | convolution fusion | flops 805306368 | bytes 3145728 | tf_op jit(solution)/shard_map/aij,ajk->aik/dot_general | solution.py:35
  67.9 1.4 %fusion.16 = f32[4,256,256]{2,1,0:T(8,128)S(1)} fusion(f32[4,256,256]{2,1,0:T(8,128)S(1)} %fusion.80, f32[4,256,256]{2,1,0:T(8,128)S(1)} %fusion.81, f32[256,256]{1,0:T(8,128)S(1)} %fusion.53), kind=kOutput, calls=%fused_computation.26 | convolution fusion | flops 805830656 | bytes 3407872 | tf_op jit(solution)/shard_map/aij,ajk->aik/dot_general | solution.py:31
  72.7 2.3 %collective-permute-start = (bf16[1,4,256,256]{3,2,1,0:T(8,128)(2,1)S(1)}, bf16[1,4,256,256]{3,2,1,0:T(8,128)(2,1)S(1)}, u32[]{:S(2)}, u32[]{:S(2)}) collective-permute-start(bf16[1,4,256,256]{3,2,1,0:T(8,128)(2,1)S(1)} %fusion.45), channel_id=1, source_target_pairs={{0,1},{1,2},{2,3},{4,5},{5,6},{6,7},{8,9},{9,10},{10,11},{12,13},{... | collective-permute-start | bytes 1572872 | tf_op jit(solution)/shard_map/ppermute | solution.py:16
  75.0 1.3 %collective-permute-start.1 = (bf16[1,4,256,256]{3,2,1,0:T(8,128)(2,1)S(1)}, bf16[1,4,256,256]{3,2,1,0:T(8,128)(2,1)S(1)}, u32[]{:S(2)}, u32[]{:S(2)}) collective-permute-start(bf16[1,4,256,256]{3,2,1,0:T(8,128)(2,1)S(1)} %fusion.45), channel_id=1, source_target_pairs={{1,0},{2,1},{3,2},{5,4},{6,5},{7,6},{9,8},{10,9},{11,10},{13,12},{... | collective-permute-start | bytes 1572872 | tf_op jit(solution)/shard_map/ppermute | solution.py:19
  77.0 4.1 %all-to-all-start = ((bf16[64,4,512]{2,0,1:T(8,128)(2,1)}), bf16[64,4,512]{2,0,1:T(8,128)(2,1)S(1)}, u32[]{:S(2)}, u32[]{:S(2)}) async-start(bf16[64,4,512]{2,0,1:T(8,128)(2,1)} %bitcast.73), calls=%async_computation | async-start | bytes 524288 | tf_op jit(solution)/shard_map/all_to_all | solution.py:86
  81.7 7.4 %all-to-all-done = bf16[64,4,512]{2,0,1:T(8,128)(2,1)S(1)} async-done(((bf16[64,4,512]{2,0,1:T(8,128)(2,1)}), bf16[64,4,512]{2,0,1:T(8,128)(2,1)S(1)}, u32[]{:S(2)}, u32[]{:S(2)}) %all-to-all-start) | async-done | bytes 262176 | tf_op jit(solution)/shard_map/all_to_all | solution.py:86
  90.7 2.0 %gather_fusion.3 = bf16[16,256,256]{2,1,0:T(8,128)(2,1)} fusion(bf16[12,256,256]{2,1,0:T(8,128)(2,1)S(1)} %bitcast.77, s32[1024]{0:T(1024)S(1)} %pad_clamp_fusion.2), kind=kCustom, calls=%fused_computation.1.clone | custom fusion | bytes 4194368 | tf_op jit(solution)/shard_map/jit(_take)/gather | solution.py:99
  92.7 2.0 %gather_fusion.4 = bf16[16,256,256]{2,1,0:T(8,128)(2,1)} fusion(bf16[12,256,256]{2,1,0:T(8,128)(2,1)S(1)} %bitcast.78, s32[1024]{0:T(1024)S(1)} %pad_clamp_fusion.1), kind=kCustom, calls=%fused_computation.2.clone | custom fusion | bytes 4194368 | tf_op jit(solution)/shard_map/jit(_take)/gather | solution.py:99
  94.7 2.0 %gather_fusion.5 = bf16[16,256,256]{2,1,0:T(8,128)(2,1)} fusion(bf16[12,256,256]{2,1,0:T(8,128)(2,1)S(1)} %bitcast.79, s32[1024]{0:T(1024)S(1)} %pad_clamp_fusion), kind=kCustom, calls=%fused_computation.3.clone | custom fusion | bytes 4194368 | tf_op jit(solution)/shard_map/jit(_take)/gather | solution.py:99
  96.7 2.0 %gather_fusion.2 = bf16[16,256,256]{2,1,0:T(8,128)(2,1)} fusion(bf16[12,256,256]{2,1,0:T(8,128)(2,1)S(1)} %bitcast.80, s32[1024]{0:T(1024)S(1)} %pad_clamp_fusion.3), kind=kCustom, calls=%fused_computation.clone | custom fusion | bytes 4194368 | tf_op jit(solution)/shard_map/jit(_take)/gather | solution.py:99
  98.7 2.3 %fusion.29 = f32[16,32,256]{2,1,0:T(8,128)S(1)} fusion(bf16[256,16,32]{0,2,1:T(8,128)(2,1)S(1)} %subtract_convert_fusion, bf16[16,256,256]{2,1,0:T(8,128)(2,1)} %gather_fusion.3, pred[16]{0:T(512)(128)(4,1)S(1)} %compare_and_fusion.4, f32[16,32]{1,0:T(8,128)S(1)} %mul.175), kind=kOutput, calls=%fused_computation.36 | convolution fusion | flops 68288512 | bytes 2885648 | tf_op jit(solution)/shard_map/kgc,gkj->gcj/dot_general | solution.py:100
  (76 shorter events, 14.2 us)
Async XLA Ops:
  0.0 6.2 %copy-start.4 = (s32[1,1024]{1,0:T(1,128)S(1)}, s32[1,1024]{1,0:T(1,128)}, u32[]{:S(2)}) copy-start(s32[1,1024]{1,0:T(1,128)} %param.11) | copy-start | bytes 12292
  2.9 45.1 %copy-start.7 = (f32[1,1024]{1,0:T(1,128)S(1)}, f32[1,1024]{1,0:T(1,128)}, u32[]{:S(2)}) copy-start(f32[1,1024]{1,0:T(1,128)} %param.9) | copy-start | bytes 12292
  38.9 17.5 %copy-start.6 = (f32[1,4,1024]{2,1,0:T(4,128)S(1)}, f32[1,4,1024]{2,1,0:T(4,128)}, u32[]{:S(2)}) copy-start(f32[1,4,1024]{2,1,0:T(4,128)} %param.12) | copy-start | bytes 49156
  70.5 5.8 %copy-start.3 = (bf16[64,2048]{1,0:T(8,128)(2,1)S(1)}, bf16[64,2048]{1,0:T(8,128)(2,1)}, u32[]{:S(2)}) copy-start(bf16[64,2048]{1,0:T(8,128)(2,1)} %param.8) | copy-start | bytes 786436
  71.5 9.8 %copy-start.5 = (f32[4,512]{1,0:T(4,128)S(1)}, f32[4,512]{1,0:T(4,128)}, u32[]{:S(2)}) copy-start(f32[4,512]{1,0:T(4,128)} %param.13) | copy-start | bytes 24580
  72.7 17.8 %collective-permute-start = (bf16[1,4,256,256]{3,2,1,0:T(8,128)(2,1)S(1)}, bf16[1,4,256,256]{3,2,1,0:T(8,128)(2,1)S(1)}, u32[]{:S(2)}, u32[]{:S(2)}) collective-permute-start(bf16[1,4,256,256]{3,2,1,0:T(8,128)(2,1)S(1)} %fusion.45), channel_id=1, source_target_pairs={{0,1},{1,2},{2,3},{4,5},{5,6},{6,7},{8,9},{9,10},{10,11},{12,13},{... | collective-permute-start | bytes 1572872 | tf_op jit(solution)/shard_map/ppermute | solution.py:16
  75.0 15.5 %collective-permute-start.1 = (bf16[1,4,256,256]{3,2,1,0:T(8,128)(2,1)S(1)}, bf16[1,4,256,256]{3,2,1,0:T(8,128)(2,1)S(1)}, u32[]{:S(2)}, u32[]{:S(2)}) collective-permute-start(bf16[1,4,256,256]{3,2,1,0:T(8,128)(2,1)S(1)} %fusion.45), channel_id=1, source_target_pairs={{1,0},{2,1},{3,2},{5,4},{6,5},{7,6},{9,8},{10,9},{11,10},{13,12},{... | collective-permute-start | bytes 1572872 | tf_op jit(solution)/shard_map/ppermute | solution.py:19
  77.0 12.1 %all-to-all-start = ((bf16[64,4,512]{2,0,1:T(8,128)(2,1)}), bf16[64,4,512]{2,0,1:T(8,128)(2,1)S(1)}, u32[]{:S(2)}, u32[]{:S(2)}) async-start(bf16[64,4,512]{2,0,1:T(8,128)(2,1)} %bitcast.73), calls=%async_computation | async-start | bytes 524288 | tf_op jit(solution)/shard_map/all_to_all | solution.py:86
  98.7 2.3 %copy-start.2 = (bf16[16,256,256]{2,1,0:T(8,128)(2,1)S(1)}, bf16[16,256,256]{2,1,0:T(8,128)(2,1)}, u32[]{:S(2)}) copy-start(bf16[16,256,256]{2,1,0:T(8,128)(2,1)} %gather_fusion.4) | copy-start | bytes 6291460
  101.0 1.6 %copy-start.1 = (bf16[16,256,256]{2,1,0:T(8,128)(2,1)S(1)}, bf16[16,256,256]{2,1,0:T(8,128)(2,1)}, u32[]{:S(2)}) copy-start(bf16[16,256,256]{2,1,0:T(8,128)(2,1)} %gather_fusion.5) | copy-start | bytes 6291460
  101.5 1.8 %copy-start = (bf16[16,256,256]{2,1,0:T(8,128)(2,1)S(1)}, bf16[16,256,256]{2,1,0:T(8,128)(2,1)}, u32[]{:S(2)}) copy-start(bf16[16,256,256]{2,1,0:T(8,128)(2,1)} %gather_fusion.2) | copy-start | bytes 6291460
where the time goes:
time: 105 us
  blocking collectives  45.6 us (43%)
  matrix products  19.8 us (19%)
  local copies, waits for them, and re-layouts  19.4 us (18%)
  starting transfers between devices  7.71 us (7%)
  waiting for transfers between devices  7.42 us (7%)
  other arithmetic  3.57 us (3%)
  between operations  1.12 us (1%)
    all_gather x1, blocking collectives, per_device(): pieces = lax.all_gather(border, 'region', axis=1, tiled=True)  32.6 us
    gather x4, local copies, waits for them, and re-layouts, per_device(): chosen = jnp.take(stacked, chosen_index, axis=0)  8.04 us
    all_to_all x1, waiting for transfers between devices, per_device(): lax.all_to_all(ensemble, 'member', split_axis=1, concat_axis=0, tiled=True)  7.41 us
    all_gather x1, blocking collectives, per_device(): report_pert = lax.all_gather(local_pert, 'member', axis=0, tiled=True)  7.41 us
    psum x1, blocking collectives, per_device(): report_mean = lax.psum(jnp.sum(at_reports, axis=0), 'member') / members  5.67 us
    dot_general x4, matrix products, make_transform(): jnp.einsum('aij,ajk->aik', root_iter, current, precision=highest)  4.92 us
    dot_general x4, matrix products, make_transform(): root_iter = jnp.einsum('aij,ajk->aik', middle, root_iter, precision=highest)  4.53 us
    all_to_all x1, starting transfers between devices, per_device(): lax.all_to_all(ensemble, 'member', split_axis=1, concat_axis=0, tiled=True)  4.14 us
  transfers between devices with their start and end apart: 3, of which 1 were waited for; matrix products, arithmetic and copies ran while one was open for 2% of the time, Pallas kernels for 0%

commit v1 on v0

--- a/solution.py
+++ b/solution.py
@@ -70,7 +70,24 @@
     at_reports = jnp.where(is_local[None, :], local_values, remote)
     report_mean = lax.psum(jnp.sum(at_reports, axis=0), "member") / members
     local_pert = (at_reports - report_mean[None, :]).astype(jnp.bfloat16)
-    report_pert = lax.all_gather(local_pert, "member", axis=0, tiled=True)
+
+    def choose_tiles(local_block):
+        dev_axis = "member"
+        mid_arr = jax.lax.psum(1, axis_name=dev_axis)
+        latest = jax.lax.axis_index(dev_axis)
+        base_arr, val2 = (mid_arr, latest)
+        x_next, arr_out = (local_block, 1)
+        while arr_out < base_arr:
+            left_arr = jax.lax.ppermute(
+                x_next, axis_name=dev_axis, perm=[(j0, j0 ^ arr_out) for j0 in range(base_arr)]
+            )
+            inter = jnp.concatenate([x_next, left_arr], axis=0)
+            far_arr = jnp.concatenate([left_arr, x_next], axis=0)
+            x_next = jnp.where(val2 & arr_out == 0, inter, far_arr)
+            arr_out = 2 * arr_out
+        return x_next
+
+    report_pert = choose_tiles(local_pert)
     active = (jnp.arange(report_pert.shape[1]) < report_count[0]).astype(jnp.float32)
     weights = report_weight[0] * active[None, :]
     weighted = (report_pert[None, :, :] * weights[:, None, :]).astype(jnp.bfloat16)

time: 105 us -> 111 us (1.057)
  the two profiles are of different devices: /device:TPU:0 before, /device:TPU:1 now
where the time goes in v1:
time: 111 us
  blocking collectives  37.6 us (34%)
  matrix products  20.8 us (19%)
  local copies, waits for them, and re-layouts  20.2 us (18%)
  waiting for transfers between devices  14.9 us (13%)
  starting transfers between devices  10.3 us (9%)
  other arithmetic  6.03 us (5%)
  between operations  1.17 us (1%)
    all_gather x1, blocking collectives, per_device(): pieces = lax.all_gather(border, 'region', axis=1, tiled=True)  25.9 us
    psum x1, blocking collectives, per_device(): report_mean = lax.psum(jnp.sum(at_reports, axis=0), 'member') / members  11.7 us
    gather x4, local copies, waits for them, and re-layouts, per_device(): chosen = jnp.take(stacked, chosen_index, axis=0)  8.04 us
    ppermute x2, waiting for transfers between devices, choose_tiles(): jax.lax.ppermute(x_next, axis_name=dev_axis, perm=[(j0, j0 ^ arr_out) for...  5.56 us
    dot_general x4, matrix products, make_transform(): root_iter = jnp.einsum('aij,ajk->aik', middle, root_iter, precision=highest)  4.73 us
    dot_general x4, matrix products, make_transform(): jnp.einsum('aij,ajk->aik', root_iter, current, precision=highest)  4.71 us
    ppermute x1, waiting for transfers between devices, extended(): lax.ppermute(lax.slice_in_dim(block, 0, width, axis=dim), axis, backward)  4.4 us
    dot_general x4, matrix products, per_device(): jnp.einsum('kgc,gkj->gcj', anomaly_view, chosen, preferred_element_type=j...  3.83 us
  transfers between devices with their start and end apart: 5, of which 4 were waited for; matrix products, arithmetic and copies ran while one was open for 3% of the time, Pallas kernels for 0%

profile of v1, /device:TPU:1, one launch (start us, length us, event | category | flops | bytes accessed | tf_op | source)
XLA Modules:
  0.0 110.9 jit_solution(5346795213259348145)
XLA Ops:
  1.6 1.2 %copy.24 = bf16[64,2048]{0,1:T(8,128)(2,1)S(1)} copy(bf16[64,2048]{1,0:T(8,128)(2,1)} %param.8) | data formatting | bytes 524288 | tf_op args[0]
  2.8 3.2 %gather_fusion = bf16[1024,64]{1,0:T(8,128)(2,1)S(1)} fusion(bf16[64,2048]{0,1:T(8,128)(2,1)S(1)} %copy.24, s32[1024]{0:T(1024)S(1)} %broadcast_clamp_fusion.1), kind=kCustom, calls=%fused_computation.4 | custom fusion | bytes 266240 | tf_op jit(solution)/shard_map/jit(_take)/gather | solution.py:62
  6.1 25.9 %all_gather.3 = bf16[64,1024]{0,1:T(8,128)(2,1)S(1)} all-gather(bf16[64,128]{0,1:T(8,128)(2,1)S(1)} %slice.37), channel_id=1, replica_groups=mesh['region'=8,'member'=4] {'region'}, dimensions={1}, use_global_device_ids=true | all-gather | bytes 147456 | tf_op jit(solution)/shard_map/all_gather | solution.py:65
  32.1 3.2 %gather_fusion.1 = bf16[1024,64]{1,0:T(8,128)(2,1)S(1)} fusion(bf16[64,1024]{0,1:T(8,128)(2,1)S(1)} %all_gather.3, s32[1024]{0:T(1024)S(1)} %broadcast_clamp_fusion), kind=kCustom, calls=%fused_computation.5 | custom fusion | bytes 266240 | tf_op jit(solution)/shard_map/jit(_take)/gather | solution.py:68
  36.3 11.7 %psum.7 = f32[1024]{0:T(1024)S(1)} all-reduce(f32[1024]{0:T(1024)S(1)} %fusion.51), channel_id=1, replica_groups=mesh['region'=8,'member'=4] {'member'}, use_global_device_ids=true, to_apply=%region_3.4 | all-reduce | flops 1024 | bytes 8192 | tf_op jit(solution)/shard_map/psum | solution.py:71
  48.0 1.2 %fusion.52 = bf16[64,1024]{0,1:T(8,128)(2,1)S(1)} fusion(f32[1024]{0:T(1024)S(1)} %get-tuple-element.18, pred[1024]{0:T(1024)(128)(4,1)S(1)} %get-tuple-element.11, pred[1024]{0:T(1024)(128)(4,1)S(1)} %get-tuple-element.10, bf16[1024,64]{1,0:T(8,128)(2,1)S(1)} %gather_fusion, pred[1024]{0:T(1024)(128)(4,1)S(1)} %get-tuple-element.20, ...), kind=kLoop, calls=%fused_computation.62 | loop fusion | flops 524288 | bytes 401408 | tf_op jit(solution)/shard_map/convert_element_type | solution.py:72
  50.7 3.4 %all-to-all-start = ((bf16[64,4,512]{2,0,1:T(8,128)(2,1)}), bf16[64,4,512]{2,0,1:T(8,128)(2,1)S(1)}, u32[]{:S(2)}, u32[]{:S(2)}) async-start(bf16[64,4,512]{2,0,1:T(8,128)(2,1)} %bitcast.72), calls=%async_computation | async-start | bytes 524288 | tf_op jit(solution)/shard_map/all_to_all | solution.py:103
  55.4 1.5 %collective-permute-start.1 = (bf16[128,1024]{0,1:T(8,128)(2,1)S(1)}, bf16[128,1024]{0,1:T(8,128)(2,1)S(1)}, u32[]{:S(2)}, u32[]{:S(2)}) collective-permute-start(bf16[128,1024]{0,1:T(8,128)(2,1)S(1)} %maximum_select_fusion.1), channel_id=1, source_target_pairs={{0,2},{1,3},{2,0},{3,1},{4,6},{5,7},{6,4},{7,5},{8,10},{9,11},{10,... | collective-permute-start | bytes 786440 | tf_op jit(solution)/shard_map/ppermute | solution.py:81
  57.2 2.0 %all-to-all-done = bf16[64,4,512]{2,0,1:T(8,128)(2,1)S(1)} async-done(((bf16[64,4,512]{2,0,1:T(8,128)(2,1)}), bf16[64,4,512]{2,0,1:T(8,128)(2,1)S(1)}, u32[]{:S(2)}, u32[]{:S(2)}) %all-to-all-start) | async-done | bytes 262176 | tf_op jit(solution)/shard_map/all_to_all | solution.py:103
  59.3 5.6 %collective-permute-done.1 = bf16[128,1024]{0,1:T(8,128)(2,1)S(1)} collective-permute-done((bf16[128,1024]{0,1:T(8,128)(2,1)S(1)}, bf16[128,1024]{0,1:T(8,128)(2,1)S(1)}, u32[]{:S(2)}, u32[]{:S(2)}) %collective-permute-start.1) | collective-permute-done | bytes 262176 | tf_op jit(solution)/shard_map/ppermute | solution.py:81
  66.1 1.9 %multiply_reduce_fusion = (f32[4]{0:T(128)S(1)}, f32[4,256,256]{2,1,0:T(8,128)S(1)}) fusion(bf16[128,1024]{0,1:T(8,128)(2,1)S(1)} %maximum_select_fusion.1, bf16[128,1024]{0,1:T(8,128)(2,1)} %copy-done.4, pred[]{:T(512)S(6)} %eq.59, f32[4,1024]{1,0:T(4,128)S(1)} %bitcast_multiply_fusion, f32[256,1024]{1,0:T(8,128)S(1)} %copy.26, f32[256,256]{1,0:T(8,128)S(1)} %fusion.53), kind=kOutput, calls=%fused_computation.46 | convolution fusion | flops 542113792 | bytes 2899985 | tf_op jit(solution)/shard_map/ako,jo->akj/dot_general | solution.py:95
  69.2 1.2 %fusion.56 = f32[4,256,256]{2,1,0:T(8,128)S(1)} fusion(f32[4,256,256]{2,1,0:T(8,128)S(1)} %fusion.19, f32[4,256,256]{2,1,0:T(8,128)S(1)} %get-tuple-element.24, f32[4]{0:T(128)S(1)} %get-tuple-element.22), kind=kOutput, calls=%fused_computation.71 | convolution fusion | flops 805568512 | bytes 3145744 | tf_op jit(solution)/shard_map/aij,ajk->aik/dot_general | solution.py:34
  71.5 1.2 %fusion.18 = f32[4,256,256]{2,1,0:T(8,128)S(1)} fusion(f32[4,256,256]{2,1,0:T(8,128)S(1)} %fusion.48, f32[4,256,256]{2,1,0:T(8,128)S(1)} %fusion.56, f32[256,256]{1,0:T(8,128)S(1)} %fusion.55), kind=kOutput, calls=%fused_computation.30 | convolution fusion | flops 805830656 | bytes 3407872 | tf_op jit(solution)/shard_map/aij,ajk->aik/dot_general | solution.py:31
  75.0 1.2 %fusion.17 = f32[4,256,256]{2,1,0:T(8,128)S(1)} fusion(f32[4,256,256]{2,1,0:T(8,128)S(1)} %fusion.79, f32[4,256,256]{2,1,0:T(8,128)S(1)} %fusion.80, f32[256,256]{1,0:T(8,128)S(1)} %fusion.55), kind=kOutput, calls=%fused_computation.28 | convolution fusion | flops 805830656 | bytes 3407872 | tf_op jit(solution)/shard_map/aij,ajk->aik/dot_general | solution.py:31
  77.3 1.4 %fusion.81 = f32[4,256,256]{2,1,0:T(8,128)S(1)} fusion(f32[4,256,256]{2,1,0:T(8,128)S(1)} %fusion.17, f32[4,256,256]{2,1,0:T(8,128)S(1)} %fusion.79), kind=kOutput, calls=%fused_computation.162 | convolution fusion | flops 805306368 | bytes 3145728 | tf_op jit(solution)/shard_map/aij,ajk->aik/dot_general | solution.py:35
  83.5 2.7 %collective-permute-start.2 = (bf16[1,4,256,256]{3,2,1,0:T(8,128)(2,1)S(1)}, bf16[1,4,256,256]{3,2,1,0:T(8,128)(2,1)S(1)}, u32[]{:S(2)}, u32[]{:S(2)}) collective-permute-start(bf16[1,4,256,256]{3,2,1,0:T(8,128)(2,1)S(1)} %fusion.45), channel_id=1, source_target_pairs={{0,1},{1,2},{2,3},{4,5},{5,6},{6,7},{8,9},{9,10},{10,11},{12,13},{... | collective-permute-start | bytes 1572872 | tf_op jit(solution)/shard_map/ppermute | solution.py:16
  86.2 1.9 %collective-permute-start.3 = (bf16[1,4,256,256]{3,2,1,0:T(8,128)(2,1)S(1)}, bf16[1,4,256,256]{3,2,1,0:T(8,128)(2,1)S(1)}, u32[]{:S(2)}, u32[]{:S(2)}) collective-permute-start(bf16[1,4,256,256]{3,2,1,0:T(8,128)(2,1)S(1)} %fusion.45), channel_id=1, source_target_pairs={{1,0},{2,1},{3,2},{5,4},{6,5},{7,6},{9,8},{10,9},{11,10},{13,12},{... | collective-permute-start | bytes 1572872 | tf_op jit(solution)/shard_map/ppermute | solution.py:19
  89.4 2.9 %collective-permute-done.2 = bf16[1,4,256,256]{3,2,1,0:T(8,128)(2,1)S(1)} collective-permute-done((bf16[1,4,256,256]{3,2,1,0:T(8,128)(2,1)S(1)}, bf16[1,4,256,256]{3,2,1,0:T(8,128)(2,1)S(1)}, u32[]{:S(2)}, u32[]{:S(2)}) %collective-permute-start.2) | collective-permute-done | bytes 524320 | tf_op jit(solution)/shard_map/ppermute | solution.py:16
  92.3 4.4 %collective-permute-done.3 = bf16[1,4,256,256]{3,2,1,0:T(8,128)(2,1)S(1)} collective-permute-done((bf16[1,4,256,256]{3,2,1,0:T(8,128)(2,1)S(1)}, bf16[1,4,256,256]{3,2,1,0:T(8,128)(2,1)S(1)}, u32[]{:S(2)}, u32[]{:S(2)}) %collective-permute-start.3) | collective-permute-done | bytes 524320 | tf_op jit(solution)/shard_map/ppermute | solution.py:19
  96.9 2.0 %gather_fusion.3 = bf16[16,256,256]{2,1,0:T(8,128)(2,1)} fusion(bf16[12,256,256]{2,1,0:T(8,128)(2,1)S(1)} %bitcast.76, s32[1024]{0:T(1024)S(1)} %pad_clamp_fusion.2), kind=kCustom, calls=%fused_computation.1.clone | custom fusion | bytes 4194368 | tf_op jit(solution)/shard_map/jit(_take)/gather | solution.py:116
  98.9 2.0 %gather_fusion.4 = bf16[16,256,256]{2,1,0:T(8,128)(2,1)} fusion(bf16[12,256,256]{2,1,0:T(8,128)(2,1)S(1)} %bitcast.77, s32[1024]{0:T(1024)S(1)} %pad_clamp_fusion.1), kind=kCustom, calls=%fused_computation.2.clone | custom fusion | bytes 4194368 | tf_op jit(solution)/shard_map/jit(_take)/gather | solution.py:116
  100.8 2.0 %gather_fusion.5 = bf16[16,256,256]{2,1,0:T(8,128)(2,1)} fusion(bf16[12,256,256]{2,1,0:T(8,128)(2,1)S(1)} %bitcast.78, s32[1024]{0:T(1024)S(1)} %pad_clamp_fusion), kind=kCustom, calls=%fused_computation.3.clone | custom fusion | bytes 4194368 | tf_op jit(solution)/shard_map/jit(_take)/gather | solution.py:116
  102.9 2.0 %gather_fusion.2 = bf16[16,256,256]{2,1,0:T(8,128)(2,1)} fusion(bf16[12,256,256]{2,1,0:T(8,128)(2,1)S(1)} %bitcast.79, s32[1024]{0:T(1024)S(1)} %pad_clamp_fusion.3), kind=kCustom, calls=%fused_computation.clone | custom fusion | bytes 4194368 | tf_op jit(solution)/shard_map/jit(_take)/gather | solution.py:116
  104.9 2.3 %fusion.29 = f32[16,32,256]{2,1,0:T(8,128)S(1)} fusion(bf16[256,16,32]{0,2,1:T(8,128)(2,1)S(1)} %subtract_convert_fusion.1, bf16[16,256,256]{2,1,0:T(8,128)(2,1)} %gather_fusion.3, pred[16]{0:T(512)(128)(4,1)S(1)} %compare_and_fusion.4, f32[16,32]{1,0:T(8,128)S(1)} %mul.175), kind=kOutput, calls=%fused_computation.36 | convolution fusion | flops 68288512 | bytes 2885648 | tf_op jit(solution)/shard_map/kgc,gkj->gcj/dot_general | solution.py:117
  (83 shorter events, 21.8 us)
Async XLA Ops:
  0.0 6.0 %copy-start.6 = (s32[1,1024]{1,0:T(1,128)S(1)}, s32[1,1024]{1,0:T(1,128)}, u32[]{:S(2)}) copy-start(s32[1,1024]{1,0:T(1,128)} %param.11) | copy-start | bytes 12292
  0.0 48.0 %copy-start.9 = (f32[1,1024]{1,0:T(1,128)S(1)}, f32[1,1024]{1,0:T(1,128)}, u32[]{:S(2)}) copy-start(f32[1,1024]{1,0:T(1,128)} %param.9) | copy-start | bytes 12292
  2.8 47.2 %copy-start.3 = (bf16[64,2048]{1,0:T(8,128)(2,1)S(1)}, bf16[64,2048]{1,0:T(8,128)(2,1)}, u32[]{:S(2)}) copy-start(bf16[64,2048]{1,0:T(8,128)(2,1)} %param.8) | copy-start | bytes 786436
  6.1 48.8 %copy-start.7 = (f32[4,512]{1,0:T(4,128)S(1)}, f32[4,512]{1,0:T(4,128)}, u32[]{:S(2)}) copy-start(f32[4,512]{1,0:T(4,128)} %param.13) | copy-start | bytes 24580
  6.1 48.9 %copy-start.8 = (f32[1,4,1024]{2,1,0:T(4,128)S(1)}, f32[1,4,1024]{2,1,0:T(4,128)}, u32[]{:S(2)}) copy-start(f32[1,4,1024]{2,1,0:T(4,128)} %param.12) | copy-start | bytes 49156
  49.2 5.8 %collective-permute-start = (bf16[64,1024]{0,1:T(8,128)(2,1)S(1)}, bf16[64,1024]{0,1:T(8,128)(2,1)S(1)}, u32[]{:S(2)}, u32[]{:S(2)}) collective-permute-start(bf16[64,1024]{0,1:T(8,128)(2,1)S(1)} %fusion.52), channel_id=1, source_target_pairs={{0,1},{1,0},{2,3},{3,2},{4,5},{5,4},{6,7},{7,6},{8,9},{9,8},{10,11... | collective-permute-start | bytes 393224 | tf_op jit(solution)/shard_map/ppermute | solution.py:81
  50.7 8.6 %all-to-all-start = ((bf16[64,4,512]{2,0,1:T(8,128)(2,1)}), bf16[64,4,512]{2,0,1:T(8,128)(2,1)S(1)}, u32[]{:S(2)}, u32[]{:S(2)}) async-start(bf16[64,4,512]{2,0,1:T(8,128)(2,1)} %bitcast.72), calls=%async_computation | async-start | bytes 524288 | tf_op jit(solution)/shard_map/all_to_all | solution.py:103
  55.4 9.5 %collective-permute-start.1 = (bf16[128,1024]{0,1:T(8,128)(2,1)S(1)}, bf16[128,1024]{0,1:T(8,128)(2,1)S(1)}, u32[]{:S(2)}, u32[]{:S(2)}) collective-permute-start(bf16[128,1024]{0,1:T(8,128)(2,1)S(1)} %maximum_select_fusion.1), channel_id=1, source_target_pairs={{0,2},{1,3},{2,0},{3,1},{4,6},{5,7},{6,4},{7,5},{8,10},{9,11},{10,... | collective-permute-start | bytes 786440 | tf_op jit(solution)/shard_map/ppermute | solution.py:81
  64.9 0.7 copy-start.4
  79.9 1.2 %copy-start.5 = (bf16[128,1024]{0,1:T(8,128)(2,1)S(1)}, bf16[128,1024]{0,1:T(8,128)(2,1)}, u32[]{:S(2)}) copy-start(bf16[128,1024]{0,1:T(8,128)(2,1)} %copy-done.4) | copy-start | bytes 786436
  83.5 8.8 %collective-permute-start.2 = (bf16[1,4,256,256]{3,2,1,0:T(8,128)(2,1)S(1)}, bf16[1,4,256,256]{3,2,1,0:T(8,128)(2,1)S(1)}, u32[]{:S(2)}, u32[]{:S(2)}) collective-permute-start(bf16[1,4,256,256]{3,2,1,0:T(8,128)(2,1)S(1)} %fusion.45), channel_id=1, source_target_pairs={{0,1},{1,2},{2,3},{4,5},{5,6},{6,7},{8,9},{9,10},{10,11},{12,13},{... | collective-permute-start | bytes 1572872 | tf_op jit(solution)/shard_map/ppermute | solution.py:16
  86.2 10.5 %collective-permute-start.3 = (bf16[1,4,256,256]{3,2,1,0:T(8,128)(2,1)S(1)}, bf16[1,4,256,256]{3,2,1,0:T(8,128)(2,1)S(1)}, u32[]{:S(2)}, u32[]{:S(2)}) collective-permute-start(bf16[1,4,256,256]{3,2,1,0:T(8,128)(2,1)S(1)} %fusion.45), channel_id=1, source_target_pairs={{1,0},{2,1},{3,2},{5,4},{6,5},{7,6},{9,8},{10,9},{11,10},{13,12},{... | collective-permute-start | bytes 1572872 | tf_op jit(solution)/shard_map/ppermute | solution.py:19
  104.9 2.3 %copy-start.2 = (bf16[16,256,256]{2,1,0:T(8,128)(2,1)S(1)}, bf16[16,256,256]{2,1,0:T(8,128)(2,1)}, u32[]{:S(2)}) copy-start(bf16[16,256,256]{2,1,0:T(8,128)(2,1)} %gather_fusion.4) | copy-start | bytes 6291460
  107.2 1.6 %copy-start.1 = (bf16[16,256,256]{2,1,0:T(8,128)(2,1)S(1)}, bf16[16,256,256]{2,1,0:T(8,128)(2,1)}, u32[]{:S(2)}) copy-start(bf16[16,256,256]{2,1,0:T(8,128)(2,1)} %gather_fusion.5) | copy-start | bytes 6291460
  107.7 1.8 %copy-start = (bf16[16,256,256]{2,1,0:T(8,128)(2,1)S(1)}, bf16[16,256,256]{2,1,0:T(8,128)(2,1)}, u32[]{:S(2)}) copy-start(bf16[16,256,256]{2,1,0:T(8,128)(2,1)} %gather_fusion.2) | copy-start | bytes 6291460
